TPU v7x, 32 devices: a whole 2x2x4 slice. The times are simulated.
32 devices in a mesh: ctx: 8 (over z, y), head: 4 (over x, core).
Axes of the slice: x: 2, y: 2, z: 4, core: 2. Of those that a mesh axis runs over, the one named last changes fastest.
Arguments:
- query_rows: bfloat16 [8192, 4096], P('ctx', 'head'), may hold values from -6 to 6
- key_rows: bfloat16 [8192, 4096], P('ctx', 'head'), may hold values from -6 to 6
- value_rows: bfloat16 [8192, 4096], P('ctx', 'head'), may hold values from -6 to 6
- level_gate: float32 [6, 32, 8192], P(None, 'head', 'ctx'), may hold values from 0 to 2.5, as said below
- out_weight: bfloat16 [4096, 4096], P('head'), may hold values from -0.09375 to 0.09375
Outputs:
- output: bfloat16 [8192, 4096], P(('ctx', 'head'))
Inputs may be any that keep to these rules, and one draw needn't show every extreme that they name: `level_gate`: every gate weight is positive.
All inputs are finite; a program needn't handle non-finite values.
Results may differ from a plain program's by a relative error of at most 0.015.
Values may be sent and summed in bfloat16 or wider, within the bound.
A program may use at most 128 MiB of HBM per device.

v0:
```python
import jax
import jax.numpy as jnp
from jax import lax
from jax.sharding import PartitionSpec as P

C = 256


EPS = 1e-06


def swapped(x, axis, bit):
    return lax.ppermute(x, axis, [(i, i ^ 1 << bit) for i in range(lax.axis_size(axis))])


def on_device(query_rows, key_rows, value_rows, level_gate, out_weight):
    tokens = query_rows.shape[0]
    local_heads = level_gate.shape[1]
    width = query_rows.shape[1] // local_heads
    stretches = tokens // C
    stretch_bits = stretches.bit_length() - 1
    ctx_bits = lax.axis_size("ctx").bit_length() - 1
    query_stretches = query_rows.reshape(stretches, C, local_heads, width)
    key_stretches = key_rows.reshape(stretches, C, local_heads, width)
    value_stretches = value_rows.reshape(stretches, C, local_heads, width)
    gate_rows = jnp.transpose(level_gate, (0, 2, 1)).reshape(
        level_gate.shape[0], stretches, C, local_heads, 1
    )
    scores = jnp.einsum(
        "cthi,cshi->chts", query_stretches, key_stretches, preferred_element_type=jnp.float32
    )
    row_ids = lax.broadcasted_iota(jnp.int32, (C, C), 0)
    col_ids = lax.broadcasted_iota(jnp.int32, (C, C), 1)
    first_gate = jnp.transpose(gate_rows[0][..., 0], (0, 2, 1))[:, :, :, None]
    weights = (jnp.where(row_ids >= col_ids, scores, 0.0) * first_gate).astype(jnp.bfloat16)
    combined = jnp.einsum(
        "chts,cshj->cthj", weights, value_stretches, preferred_element_type=jnp.float32
    )
    stretch_state = jnp.einsum(
        "cshi,cshj->chij", key_stretches, value_stretches, preferred_element_type=jnp.float32
    )
    stretch_ids = jnp.arange(stretches, dtype=jnp.int32)
    for level_bit in range(stretch_bits):
        span_size = 2**level_bit
        grouped = stretch_state.reshape(
            stretches // span_size, span_size, local_heads, width, width
        ).sum(axis=1)
        owner_block = stretch_ids // span_size
        block_ids = jnp.arange(stretches // span_size, dtype=jnp.int32)
        picker = (
            (owner_block[:, None] - 1 == block_ids[None, :]) & (owner_block[:, None] % 2 == 1)
        ).astype(jnp.float32)
        bucket = jnp.einsum(
            "cb,bhij->chij", picker, grouped, precision=lax.Precision.HIGHEST
        ).astype(jnp.bfloat16)
        readout = jnp.einsum(
            "cthi,chij->cthj", query_stretches, bucket, preferred_element_type=jnp.float32
        )
        combined = combined + readout * gate_rows[level_bit + 1]
    device_total = stretch_state.sum(axis=0)
    my_index = lax.axis_index("ctx")
    far_states = []
    running = device_total
    for level_bit in range(ctx_bits):
        partner = swapped(running.astype(jnp.bfloat16), "ctx", level_bit).astype(running.dtype)
        digit = (my_index // 2**level_bit % 2).astype(jnp.float32)
        far_states.append(partner * digit)
        running = running + partner
    for level_bit in range(ctx_bits):
        bucket = far_states[level_bit].astype(jnp.bfloat16)
        readout = jnp.einsum(
            "cthi,hij->cthj", query_stretches, bucket, preferred_element_type=jnp.float32
        )
        combined = combined + readout * gate_rows[stretch_bits + 1 + level_bit]
    normed = (
        combined * lax.rsqrt(jnp.mean(combined * combined, axis=-1, keepdims=True) + EPS)
    ).astype(jnp.bfloat16)
    normed = normed.reshape(tokens, local_heads * width)
    partial_sum = jnp.dot(normed, out_weight, preferred_element_type=jnp.float32)
    return lax.psum_scatter(
        lax.optimization_barrier(partial_sum.astype(jnp.bfloat16))
        .astype(jnp.float32)
        .astype(jnp.bfloat16),
        "head",
        scatter_dimension=0,
        tiled=True,
    )


def solution(mesh):
    in_specs = (
        P("ctx", "head"),
        P("ctx", "head"),
        P("ctx", "head"),
        P(None, "head", "ctx"),
        P("head", None),
    )
    out_specs = P(("ctx", "head"), None)
    return jax.shard_map(
        on_device, mesh=mesh, in_specs=in_specs, out_specs=out_specs, check_vma=False
    )
```

profile of v0, /device:TPU:0, one launch (start us, length us, event | category | flops | bytes accessed | tf_op | source)
XLA Modules:
  0.0 165.8 jit_solution(13408652785158061492)
XLA Ops:
  6.5 0.0 reduce-scatter.2.cloned.1.call-start
  6.5 3.5 %copy.65 = bf16[128,8,8,128]{3,2,1,0:T(8,128)(2,1)} copy(bf16[128,8,8,128]{3,1,2,0:T(8,128)(2,1)} %bitcast.88) | data formatting | bytes 4194304
  10.1 3.0 %copy.48 = bf16[4,256,8,128]{1,3,2,0:T(8,128)(2,1)S(1)} copy(bf16[4,256,8,128]{3,2,1,0:T(8,128)(2,1)} %bitcast.87) | data formatting | bytes 4194304 | tf_op jit(solution)/shard_map/reshape | solution.py:24
  13.1 0.0 copy-start.2
  13.1 3.0 %copy.66 = bf16[128,8,8,128]{3,2,1,0:T(8,128)(2,1)S(1)} copy(bf16[128,8,8,128]{3,1,2,0:T(8,128)(2,1)} %bitcast.89) | data formatting | bytes 4194304
  16.1 2.1 %fusion.64 = (f32[8,128,128]{2,1,0:T(8,128)S(1)}, f32[4,8,128,128]{3,2,1,0:T(8,128)}) fusion(bf16[4,256,8,128]{1,3,2,0:T(8,128)(2,1)S(1)} %copy.48, bf16[4,256,8,128]{3,2,1,0:T(8,128)(2,1)S(1)} %bitcast.85), kind=kOutput, calls=%fused_computation.83 | convolution fusion | flops 268828672 | bytes 6815744 | tf_op jit(solution)/shard_map/cshi,cshj->chij/dot_general | solution.py:39
  18.2 0.2 copy.56
  18.4 3.1 %collective-permute-start = (bf16[8,128,128]{1,2,0:T(8,128)(2,1)S(1)}, bf16[8,128,128]{1,2,0:T(8,128)(2,1)S(1)}, u32[]{:S(2)}, u32[]{:S(2)}) collective-permute-start(bf16[8,128,128]{1,2,0:T(8,128)(2,1)S(1)} %convert_element_type.58), channel_id=1, source_target_pairs={{0,4},{4,0},{8,12},{12,8},{16,20},{20,16},{24,28},{28,24},{1,5},{5... | collective-permute-start | bytes 786440 | tf_op jit(solution)/shard_map/ppermute | solution.py:13
  21.6 0.0 copy-done.4
  21.6 0.0 copy-start
  21.6 2.4 %copy.64 = bf16[128,8,8,128]{3,2,1,0:T(8,128)(2,1)S(1)} copy(bf16[128,8,8,128]{3,1,2,0:T(8,128)(2,1)} %bitcast.90) | data formatting | bytes 4194304
  24.0 0.1 bitcast_reduce_fusion
  24.1 3.1 %convolution_convert_fusion.1 = bf16[4,8,128,128]{3,0,2,1:T(4,128)(2,1)S(1)} fusion(f32[2,8,128,128]{3,2,1,0:T(8,128)S(1)} %bitcast_reduce_fusion, pred[4]{0:T(512)(128)(4,1)S(1)} %fusion.59, s32[4]{0:T(128)S(1)} %broadcast_add_fusion), kind=kOutput, calls=%fused_computation.28 | convolution fusion | flops 13107216 | bytes 2097172 | tf_op jit(solution)/shard_map/cb,bhij->chij/dot_general | solution.py:53
  27.3 2.7 %fusion.21 = f32[4,8,128,256]{3,2,1,0:T(8,128)} fusion(bf16[4,8,128,128]{3,0,2,1:T(4,128)(2,1)S(1)} %convolution_convert_fusion.1, bf16[4,256,8,128]{3,2,1,0:T(8,128)(2,1)S(1)} %bitcast.79), kind=kOutput, calls=%fused_computation.29 | convolution fusion | flops 268435456 | bytes 7340032 | tf_op jit(solution)/shard_map/cthi,chij->cthj/dot_general | solution.py:56
  30.0 6.8 %fusion = f32[4,8,256,128]{2,3,1,0:T(8,128)} fusion(f32[4,8,256]{2,1,0:T(8,128)S(1)} %bitcast.98, pred[256,256]{1,0:T(8,128)(4,1)S(1)} %iota_compare_fusion, bf16[4,256,8,128]{1,3,2,0:T(8,128)(2,1)} %copy-done.2, bf16[4,256,8,128]{3,2,1,0:T(8,128)(2,1)} %bitcast.86, bf16[4,256,8,128]{3,2,1,0:T(8,128)(2,1)S(1)} %bitcast.80), kind=kOutput, calls=%fused_computation.2 | convolution fusion | flops 1080033280 | bytes 10584064 | tf_op jit(solution)/shard_map/chts,cshj->cthj/dot_general | solution.py:36
  36.8 4.9 %fusion.18 = bf16[4,8,128,128]{3,0,2,1:T(4,128)(2,1)S(1)} fusion(f32[4,8,128,128]{3,2,1,0:T(8,128)} %get-tuple-element.12, s32[4]{0:T(128)S(1)} %iota_add_fusion, pred[4]{0:T(512)(128)(4,1)S(1)} %fusion.58), kind=kOutput, calls=%fused_computation.27 | convolution fusion | flops 25690144 | bytes 3145748 | tf_op jit(solution)/shard_map/cb,bhij->chij/dot_general | solution.py:53
  41.7 0.8 fusion.24
  42.4 0.0 collective-permute-done
  42.5 0.1 fusion.38
  42.5 1.6 collective-permute-start.1
  44.1 0.7 fusion.29
  44.9 5.5 %collective-permute-done.1 = bf16[8,128,128]{1,2,0:T(8,128)(2,1)S(1)} collective-permute-done((bf16[8,128,128]{1,2,0:T(8,128)(2,1)S(1)}, bf16[8,128,128]{1,2,0:T(8,128)(2,1)S(1)}, u32[]{:S(2)}, u32[]{:S(2)}) %collective-permute-start.1) | collective-permute-done | bytes 262176 | tf_op jit(solution)/shard_map/ppermute | solution.py:13
  50.3 0.1 fusion.37
  50.4 2.7 %collective-permute-start.2 = (bf16[8,128,128]{1,2,0:T(8,128)(2,1)S(1)}, bf16[8,128,128]{1,2,0:T(8,128)(2,1)S(1)}, u32[]{:S(2)}, u32[]{:S(2)}) collective-permute-start(bf16[8,128,128]{1,2,0:T(8,128)(2,1)S(1)} %fusion.37), channel_id=1, source_target_pairs={{0,16},{4,20},{8,24},{12,28},{16,0},{20,4},{24,8},{28,12},{1,17},{... | collective-permute-start | bytes 786440 | tf_op jit(solution)/shard_map/ppermute | solution.py:13
  53.1 2.7 %fusion.27 = f32[8,128,4,256]{3,1,0,2:T(8,128)} fusion(bf16[4,256,8,128]{3,2,1,0:T(8,128)(2,1)S(1)} %bitcast.83, bf16[8,128,128]{1,2,0:T(8,128)(2,1)S(1)} %collective-permute-done.1, f32[]{:T(128)S(6)} %convert_element_type.64), kind=kOutput, calls=%fused_computation.35 | convolution fusion | flops 268828672 | bytes 6553604 | tf_op jit(solution)/shard_map/cthi,hij->cthj/dot_general | solution.py:71
  55.8 8.1 %collective-permute-done.2 = bf16[8,128,128]{1,2,0:T(8,128)(2,1)S(1)} collective-permute-done((bf16[8,128,128]{1,2,0:T(8,128)(2,1)S(1)}, bf16[8,128,128]{1,2,0:T(8,128)(2,1)S(1)}, u32[]{:S(2)}, u32[]{:S(2)}) %collective-permute-start.2) | collective-permute-done | bytes 262176 | tf_op jit(solution)/shard_map/ppermute | solution.py:13
  63.9 4.8 %multiply_reduce_fusion = (f32[4,256,8]{1,2,0:T(8,128)S(1)}, f32[4,256,8,128]{1,3,2,0:T(8,128)S(1)}) fusion(f32[4,256,8]{1,2,0:T(8,128)S(1)} %bitcast.94, bf16[4,256,8,128]{3,2,1,0:T(8,128)(2,1)S(1)} %bitcast.84, bf16[8,128,128]{1,2,0:T(8,128)(2,1)S(1)} %collective-permute-done.2, f32[]{:T(128)S(6)} %convert_element_type.68, f32[4,256,8]{1,2,0:T(8,128)S(1)} %bitcast.95, ...), kind=kOutput, calls=%fused_computation.14 | convolution fusion | flops 281403392 | bytes 27721732 | tf_op jit(solution)/shard_map/cthi,hij->cthj/dot_general | solution.py:71
  68.8 0.6 multiply_convert_fusion.2
  69.4 2.6 %copy.61 = bf16[4,256,8,128]{3,2,1,0:T(8,128)(2,1)} copy(bf16[4,256,8,128]{1,3,2,0:T(8,128)(2,1)S(1)} %multiply_convert_fusion.2) | data formatting | bytes 4194304 | tf_op jit(solution)/shard_map/convert_element_type | solution.py:77
  71.9 14.7 %convolution_convert_fusion = bf16[1024,4096]{1,0:T(8,128)(2,1)} fusion(bf16[1024,4096]{1,0:T(8,128)(2,1)} %param.9, bf16[128,8,8,128]{3,2,1,0:T(8,128)(2,1)} %bitcast.91), kind=kOutput, calls=%fused_computation.1 | convolution fusion | flops 8594128896 | bytes 18874368 | tf_op jit(solution)/shard_map/dot_general | solution.py:79
  86.7 0.0 reduce-scatter.2.cloned.1.call-update
  86.7 72.3 %reduce-scatter.2.cloned.1.call-done = bf16[256,4096]{1,0:T(8,128)(2,1)} async-done(((bf16[1024,4096]{1,0:T(8,128)(2,1)}), bf16[256,4096]{1,0:T(8,128)(2,1)}) %reduce-scatter.2.cloned.1.call-update) | async-done | bytes 2097168 | tf_op jit(solution)/shard_map/reduce_scatter | solution.py:80
  (15 shorter events, 0.1 us)
Async XLA Ops:
  6.5 152.4 %reduce-scatter.2.cloned.1.call-start = ((), (), s32[]{:S(2)}) async-start(), calls=%async_computation.1 | async-start | bytes 10485760 | tf_op jit(solution)/shard_map/reduce_scatter | solution.py:80
  13.1 3.0 %copy-start.2 = (bf16[4,256,8,128]{1,3,2,0:T(8,128)(2,1)}, bf16[4,256,8,128]{1,3,2,0:T(8,128)(2,1)S(1)}, u32[]{:S(2)}) copy-start(bf16[4,256,8,128]{1,3,2,0:T(8,128)(2,1)S(1)} %copy.48) | copy-start | bytes 6291460
  16.1 2.1 %copy-start.3 = (bf16[128,8,8,128]{3,2,1,0:T(8,128)(2,1)}, bf16[128,8,8,128]{3,2,1,0:T(8,128)(2,1)S(1)}, u32[]{:S(2)}) copy-start(bf16[128,8,8,128]{3,2,1,0:T(8,128)(2,1)S(1)} %copy.66) | copy-start | bytes 6291460
  18.2 3.4 %copy-start.4 = (f32[6,8,1024]{2,1,0:T(8,128)S(1)}, f32[6,8,1024]{2,1,0:T(8,128)}, u32[]{:S(2)}) copy-start(f32[6,8,1024]{2,1,0:T(8,128)} %param.8) | copy-start | bytes 589828
  18.4 24.0 %collective-permute-start = (bf16[8,128,128]{1,2,0:T(8,128)(2,1)S(1)}, bf16[8,128,128]{1,2,0:T(8,128)(2,1)S(1)}, u32[]{:S(2)}, u32[]{:S(2)}) collective-permute-start(bf16[8,128,128]{1,2,0:T(8,128)(2,1)S(1)} %convert_element_type.58), channel_id=1, source_target_pairs={{0,4},{4,0},{8,12},{12,8},{16,20},{20,16},{24,28},{28,24},{1,5},{5... | collective-permute-start | bytes 786440 | tf_op jit(solution)/shard_map/ppermute | solution.py:13
  21.6 2.4 %copy-start = (f32[4,8,128,128]{3,2,1,0:T(8,128)S(1)}, f32[4,8,128,128]{3,2,1,0:T(8,128)}, u32[]{:S(2)}) copy-start(f32[4,8,128,128]{3,2,1,0:T(8,128)} %get-tuple-element.12) | copy-start | bytes 6291460
  42.5 7.8 %collective-permute-start.1 = (bf16[8,128,128]{1,2,0:T(8,128)(2,1)S(1)}, bf16[8,128,128]{1,2,0:T(8,128)(2,1)S(1)}, u32[]{:S(2)}, u32[]{:S(2)}) collective-permute-start(bf16[8,128,128]{1,2,0:T(8,128)(2,1)S(1)} %fusion.38), channel_id=1, source_target_pairs={{0,8},{4,12},{8,0},{12,4},{16,24},{20,28},{24,16},{28,20},{1,9},{5... | collective-permute-start | bytes 786440 | tf_op jit(solution)/shard_map/ppermute | solution.py:13
  50.4 13.5 %copy-start.1 = (f32[4,8,128,256]{3,2,1,0:T(8,128)S(1)}, f32[4,8,128,256]{3,2,1,0:T(8,128)}, u32[]{:S(2)}) copy-start(f32[4,8,128,256]{3,2,1,0:T(8,128)} %fusion.21) | copy-start | bytes 12582916
  50.4 13.5 %collective-permute-start.2 = (bf16[8,128,128]{1,2,0:T(8,128)(2,1)S(1)}, bf16[8,128,128]{1,2,0:T(8,128)(2,1)S(1)}, u32[]{:S(2)}, u32[]{:S(2)}) collective-permute-start(bf16[8,128,128]{1,2,0:T(8,128)(2,1)S(1)} %fusion.37), channel_id=1, source_target_pairs={{0,16},{4,20},{8,24},{12,28},{16,0},{20,4},{24,8},{28,12},{1,17},{... | collective-permute-start | bytes 786440 | tf_op jit(solution)/shard_map/ppermute | solution.py:13
Sparse Core Ops, SparseCore 0:
  86.8 72.0 reduce-scatter.1
where the time goes:
time: 166 us
  waiting for transfers between devices  85.8 us (52%)
  matrix products  43.4 us (26%)
  local copies, waits for them, and re-layouts  14.7 us (9%)
  between operations  13.6 us (8%)
  starting transfers between devices  7.36 us (4%)
    reduce_scatter x1, waiting for transfers between devices, on_device(): lax.psum_scatter(lax.optimization_barrier(partial_sum.astype(jnp.bfloat16...  72.3 us
    dot_general x1, matrix products, on_device(): jnp.dot(normed, out_weight, preferred_element_type=jnp.float32)  14.7 us
    ppermute x3, waiting for transfers between devices, swapped(): lax.ppermute(x, axis, [(i, i ^ 1 << bit) for i in range(lax.axis_size(axi...  13.6 us
    unnamed x13, local copies, waits for them, and re-layouts  8.89 us
    dot_general x3, matrix products, on_device(): jnp.einsum('cthi,hij->cthj', query_stretches, bucket, preferred_element_t...  8.25 us
    dot_general x2, matrix products, on_device(): jnp.einsum('cb,bhij->chij', picker, grouped, precision=lax.Precision.HIGH...  8.03 us
    ppermute x3, starting transfers between devices, swapped(): lax.ppermute(x, axis, [(i, i ^ 1 << bit) for i in range(lax.axis_size(axi...  7.35 us
    dot_general x1, matrix products, on_device(): jnp.einsum('chts,cshj->cthj', weights, value_stretches, preferred_element...  6.83 us
  transfers between devices with their start and end apart: 4, of which 3 were waited for; matrix products, arithmetic and copies ran while one was open for 15% of the time, Pallas kernels for 0%

commit v1 on v0

v1 whole, which is shorter than its diff:
```python
import functools

import jax
import jax.numpy as jnp
from jax import lax
from jax.experimental import pallas as pl
from jax.experimental.pallas import tpu as pltpu
from jax.sharding import PartitionSpec as P

C = 256
EPS = 1e-06
CHUNKS = 4
TILE = 512
MESH = pl.DeviceIdType.MESH
F32 = jnp.float32
BF16 = jnp.bfloat16


def buckets_of(stretches):
    keys = []
    span = 1
    while span < stretches:
        keys += [(span, block) for block in range(0, stretches // span, 2)]
        span *= 2
    return keys


def kernel(
    ctx_bits, heads, levels,
    q_hbm, k_hbm, v_hbm, g_hbm, w_hbm, out_hbm,
    q, k, v, g, gate_cols, w, comb, run, near, s_buf, r_buf,
    to_sib, from_sib, mine, p_send, p_recv, own, o_buf,
    load_sem, st_send, st_recv, w_send, w_recv, n_send, n_recv, p_ssem, p_rsem, o_sem,
):
    tokens, width = q.shape[0], q.shape[1] // heads
    stretches = tokens // C
    bits = stretches.bit_length() - 1
    per = heads // CHUNKS
    rows = own.shape[0]
    tiles = p_send.shape[0]
    keys = buckets_of(stretches)
    me = lax.axis_index("ctx")
    head_at = lax.axis_index("head")
    digits = [lax.rem(lax.div(me, 2**b), 2) for b in range(ctx_bits)]
    partners = [{"ctx": me + (1 - 2 * digits[b]) * 2**b} for b in range(ctx_bits)]
    core = lax.rem(head_at, 2)
    pair = lax.div(head_at, 2)
    sib = {"head": pair * 2 + 1 - core}
    far_dev = {"head": (1 - pair) * 2 + core}

    loads = [
        pltpu.make_async_copy(src, dst, load_sem.at[n])
        for n, (src, dst) in enumerate(
            ((k_hbm, k), (v_hbm, v), (q_hbm, q), (g_hbm, g), (w_hbm, w.at[0]))
        )
    ]
    for copy in loads:
        copy.start()

    barrier = pltpu.get_barrier_semaphore()
    everyone = partners + [sib, far_dev]
    for device in everyone:
        pl.semaphore_signal(barrier, inc=1, device_id=device, device_id_type=MESH)
    pl.semaphore_wait(barrier, len(everyone))

    w_copy = pltpu.make_async_remote_copy(
        src_ref=w_hbm, dst_ref=w.at[1], send_sem=w_send, recv_sem=w_recv,
        device_id=sib, device_id_type=MESH,
    )
    w_copy.start()

    def state_copy(level, chunk):
        part = pl.ds(chunk * per, per)
        return pltpu.make_async_remote_copy(
            src_ref=s_buf.at[level, part], dst_ref=r_buf.at[level, part],
            send_sem=st_send.at[level, chunk], recv_sem=st_recv.at[level, chunk],
            device_id=partners[level], device_id_type=MESH,
        )

    def service(level, chunk):
        state_copy(level, chunk).wait_recv()
        if level + 1 < ctx_bits:
            part = pl.ds(chunk * per, per)
            total = run[part] + r_buf[level, part].astype(F32)
            run[part] = total
            s_buf[level + 1, part] = total.astype(BF16)
            state_copy(level + 1, chunk).start()

    def lanes(head):
        return pl.ds(pl.multiple_of(head * width, width), width)

    loads[0].wait()
    loads[1].wait()

    @pl.loop(0, CHUNKS)
    def _(chunk):
        for inner in range(per):
            head = chunk * per + inner
            col = lanes(head)
            sums = {}
            for c in range(stretches):
                token = pl.ds(c * C, C)
                sums[1, c] = lax.dot_general(
                    k[token, col], v[token, col], (((0,), (0,)), ((), ())),
                    preferred_element_type=F32,
                )
            span = 1
            while span < stretches:
                for block in range(stretches // span // 2):
                    sums[span * 2, block] = sums[span, block * 2] + sums[span, block * 2 + 1]
                span *= 2
            for n, key in enumerate(keys):
                near[head, n] = sums[key].astype(BF16)
            run[head] = sums[stretches, 0]
            s_buf[0, head] = sums[stretches, 0].astype(BF16)
        state_copy(0, chunk).start()

    loads[2].wait()
    loads[3].wait()
    pad = gate_cols.shape[2] - levels
    for head in range(heads):
        strips = [g[level, head : head + 1, :] for level in range(levels)]
        if pad:
            strips.append(jnp.zeros((pad, tokens), F32))
        gate_cols[head] = jnp.concatenate(strips, axis=0).T

    keep = lax.broadcasted_iota(jnp.int32, (C, C), 0) >= lax.broadcasted_iota(
        jnp.int32, (C, C), 1
    )

    @pl.loop(0, CHUNKS)
    def _(chunk):
        for inner in range(per):
            head = chunk * per + inner
            col = lanes(head)
            for c in range(stretches):
                token = pl.ds(c * C, C)
                gates = gate_cols[head, token, :]
                query = q[token, col]
                scores = lax.dot_general(
                    query, k[token, col], (((1,), (1,)), ((), ())), preferred_element_type=F32
                )
                weights = (jnp.where(keep, scores, 0.0) * gates[:, 0:1]).astype(BF16)
                total = jnp.dot(weights, v[token, col], preferred_element_type=F32)
                for b in range(bits):
                    block = c // 2**b
                    if block % 2:
                        read = jnp.dot(
                            query, near[head, keys.index((2**b, block - 1))],
                            preferred_element_type=F32,
                        )
                        total = total + read * gates[:, b + 1 : b + 2]
                comb[token, col] = total
        for level in range(ctx_bits - 1):
            if level == 0:
                service(0, chunk)
            else:
                @pl.when(chunk >= level)
                def _():
                    service(level, chunk - level)

    for step in range(CHUNKS, CHUNKS + ctx_bits - 2):
        for level in range(1, ctx_bits - 1):
            if 0 <= step - level < CHUNKS:
                service(level, step - level)

    for chunk in range(CHUNKS):
        service(ctx_bits - 1, chunk)

    scale = [digit.astype(F32) for digit in digits]

    def finish(block, dst):
        token = pl.ds(pl.multiple_of(block * rows, rows), rows)

        @pl.loop(0, heads // 2)
        def _(half):
            for inner in range(2):
                head = half * 2 + inner
                col = lanes(head)
                gates = gate_cols[head, token, :]
                query = q[token, col]
                total = comb[token, col]
                for level in range(ctx_bits):
                    read = jnp.dot(query, r_buf[level, head], preferred_element_type=F32)
                    at = bits + 1 + level
                    total = total + read * (gates[:, at : at + 1] * scale[level])
                mean = jnp.mean(total * total, axis=-1, keepdims=True)
                dst[:, col] = (total * lax.rsqrt(mean + EPS)).astype(BF16)

    def sib_copy(n):
        return pltpu.make_async_remote_copy(
            src_ref=to_sib.at[n], dst_ref=from_sib.at[n],
            send_sem=n_send.at[n], recv_sem=n_recv.at[n],
            device_id=sib, device_id_type=MESH,
        )

    def p_copy(tile):
        return pltpu.make_async_remote_copy(
            src_ref=p_send.at[tile], dst_ref=p_recv.at[tile],
            send_sem=p_ssem.at[tile], recv_sem=p_rsem.at[tile],
            device_id=far_dev, device_id_type=MESH,
        )

    def out_copy(tile):
        at = pl.ds(pl.multiple_of(tile * TILE, TILE), TILE)
        return pltpu.make_async_copy(o_buf.at[:, at], out_hbm.at[:, at], o_sem.at[tile])

    def project(n, tile):
        at = pl.ds(pl.multiple_of(tile * TILE, TILE), TILE)
        return jnp.dot(mine[n], w[0, :, at], preferred_element_type=F32) + jnp.dot(
            from_sib[n], w[1, :, at], preferred_element_type=F32
        )

    other = 1 - pair
    finish(other * 2 + 1 - core, to_sib.at[0])
    sib_copy(0).start()
    finish(other * 2 + core, mine.at[0])
    loads[4].wait()
    w_copy.wait_recv()
    sib_copy(0).wait_recv()

    @pl.loop(0, tiles)
    def _(tile):
        p_send[tile] = project(0, tile).astype(BF16)
        p_copy(tile).start()

    finish(pair * 2 + 1 - core, to_sib.at[1])
    sib_copy(1).start()
    finish(pair * 2 + core, mine.at[1])
    sib_copy(1).wait_recv()

    @pl.loop(0, tiles)
    def _(tile):
        own[:, pl.ds(pl.multiple_of(tile * TILE, TILE), TILE)] = project(1, tile)

    @pl.loop(0, tiles)
    def _(tile):
        at = pl.ds(pl.multiple_of(tile * TILE, TILE), TILE)
        p_copy(tile).wait_recv()
        o_buf[:, at] = (own[:, at] + p_recv[tile].astype(F32)).astype(BF16)
        out_copy(tile).start()

    @pl.loop(0, tiles)
    def _(tile):
        p_copy(tile).wait_send()
        out_copy(tile).wait()

    for n in range(2):
        sib_copy(n).wait_send()
    w_copy.wait_send()

    @pl.loop(0, CHUNKS)
    def _(chunk):
        for level in range(ctx_bits):
            state_copy(level, chunk).wait_send()


def on_device(query_rows, key_rows, value_rows, level_gate, out_weight):
    tokens, cols = query_rows.shape
    levels, heads, _ = level_gate.shape
    width = cols // heads
    model = out_weight.shape[1]
    rows = tokens // lax.axis_size("head")
    ctx_bits = lax.axis_size("ctx").bit_length() - 1
    tiles = model // TILE
    near = len(buckets_of(tokens // C))
    dma = pltpu.SemaphoreType.DMA
    flops = 2 * tokens * cols * (model + 2 * C + width * 7)
    return pl.pallas_call(
        functools.partial(kernel, ctx_bits, heads, levels),
        out_shape=jax.ShapeDtypeStruct((rows, model), BF16),
        in_specs=[pl.BlockSpec(memory_space=pl.ANY)] * 5,
        out_specs=pl.BlockSpec(memory_space=pl.ANY),
        scratch_shapes=[
            pltpu.VMEM((tokens, cols), BF16),
            pltpu.VMEM((tokens, cols), BF16),
            pltpu.VMEM((tokens, cols), BF16),
            pltpu.VMEM((levels, heads, tokens), F32),
            pltpu.VMEM((heads, tokens, -(-levels // 8) * 8), F32),
            pltpu.VMEM((2, cols, model), BF16),
            pltpu.VMEM((tokens, cols), F32),
            pltpu.VMEM((heads, width, width), F32),
            pltpu.VMEM((heads, near, width, width), BF16),
            pltpu.VMEM((ctx_bits, heads, width, width), BF16),
            pltpu.VMEM((ctx_bits, heads, width, width), BF16),
            pltpu.VMEM((2, rows, cols), BF16),
            pltpu.VMEM((2, rows, cols), BF16),
            pltpu.VMEM((2, rows, cols), BF16),
            pltpu.VMEM((tiles, rows, TILE), BF16),
            pltpu.VMEM((tiles, rows, TILE), BF16),
            pltpu.VMEM((rows, model), F32),
            pltpu.VMEM((rows, model), BF16),
            dma((5,)),
            dma((ctx_bits, CHUNKS)),
            dma((ctx_bits, CHUNKS)),
            dma(()),
            dma(()),
            dma((2,)),
            dma((2,)),
            dma((tiles,)),
            dma((tiles,)),
            dma((tiles,)),
        ],
        compiler_params=pltpu.CompilerParams(
            collective_id=0, has_side_effects=True, vmem_limit_bytes=64 * 1024 * 1024 - 65536
        ),
        cost_estimate=pl.CostEstimate(
            flops=flops, bytes_accessed=20 * 1024 * 1024, transcendentals=tokens * heads
        ),
        name="levels_project",
    )(query_rows, key_rows, value_rows, level_gate, out_weight)


def solution(mesh):
    in_specs = (
        P("ctx", "head"),
        P("ctx", "head"),
        P("ctx", "head"),
        P(None, "head", "ctx"),
        P("head", None),
    )
    out_specs = P(("ctx", "head"), None)
    return jax.shard_map(
        on_device, mesh=mesh, in_specs=in_specs, out_specs=out_specs, check_vma=False
    )
```

time: 166 us -> 82.6 us (0.50)
  waiting for transfers between devices: 85.8 us -> 0 us
  Pallas kernels: 0 us -> 79.4 us
  matrix products: 43.4 us -> 0 us
  between operations: 13.6 us -> 0.01 us
  local copies, waits for them, and re-layouts: 14.7 us -> 3.13 us
  starting transfers between devices: 7.36 us -> 0 us
    pallas_call x0 -> x1, Pallas kernels: none -> 79.4 us  [on_device(): pl.pallas_call(functools.partial(kernel, ctx_bits, heads, levels), out_sh...]
    reduce_scatter x1 -> x0, waiting for transfers between devices: 72.3 us -> none  [on_device(): lax.psum_scatter(lax.optimization_barrier(partial_sum.astype(jnp.bfloat16...]
    dot_general x10 -> x0, matrix products: 43.4 us -> none  [the longest x1 14.7 us: on_device(): jnp.dot(normed, out_weight, preferred_element_type=jnp.float32)]
    ppermute x3 -> x0, waiting for transfers between devices: 13.6 us -> none  [swapped(): lax.ppermute(x, axis, [(i, i ^ 1 << bit) for i in range(lax.axis_size(axi...]
    ppermute x3 -> x0, starting transfers between devices: 7.35 us -> none  [swapped(): lax.ppermute(x, axis, [(i, i ^ 1 << bit) for i in range(lax.axis_size(axi...]
    unnamed x13 -> x1, local copies, waits for them, and re-layouts: 8.89 us -> 3.13 us
    reshape x1 -> x0, local copies, waits for them, and re-layouts: 2.99 us -> none  [on_device(): key_stretches = key_rows.reshape(stretches, C, local_heads, width)]
    convert_element_type x1 -> x0, local copies, waits for them, and re-layouts: 2.57 us -> none  [on_device(): normed = (combined * lax.rsqrt(jnp.mean(combined * combined, axis=-1, kee...]
  transfers between devices with their start and end apart: 4 -> 0, of which waited for: 3 -> 0; matrix products, arithmetic and copies ran while one was open for 15% -> 0% of each run, Pallas kernels for 0% -> 0%
where the time goes in v1:
time: 82.6 us; the launch traced here: 82.5 us
  Pallas kernels  79.4 us (96%)
  local copies, waits for them, and re-layouts  3.13 us (4%)
    pallas_call x1, Pallas kernels, on_device(): pl.pallas_call(functools.partial(kernel, ctx_bits, heads, levels), out_sh...  79.4 us
    unnamed x1, local copies, waits for them, and re-layouts  3.13 us

profile of v1, /device:TPU:0, one launch (start us, length us, event | category | flops | bytes accessed | tf_op | source)
XLA Modules:
  0.0 82.5 jit_solution(1132021234392940100)
XLA Ops:
  0.0 79.4 %levels_project.1 = bf16[256,4096]{1,0:T(8,128)(2,1)} custom-call(bf16[1024,1024]{1,0:T(8,128)(2,1)} %q_hbm.1, bf16[1024,1024]{1,0:T(8,128)(2,1)} %k_hbm.1, bf16[1024,1024]{1,0:T(8,128)(2,1)} %v_hbm.1, f32[6,8,1024]{2,1,0:T(8,128)} %g_hbm.1, bf16[1024,4096]{1,0:T(8,128)(2,1)} %w_hbm.1), custom_call_target="tpu_custom_call" | custom-call | flops 11542724608 | bytes 20971520 | tf_op jit(solution)/shard_map/levels_project/pallas_call | solution.py:269
  79.4 3.1 %copy.7 = bf16[256,4096]{1,0:T(8,128)(2,1)} copy(bf16[256,4096]{1,0:T(8,128)(2,1)} %levels_project.1) | data formatting | bytes 4194304

commit v2 on v1

--- a/solution.py
+++ b/solution.py
@@ -30,7 +30,7 @@
     q_hbm, k_hbm, v_hbm, g_hbm, w_hbm, out_hbm,
     q, k, v, g, gate_cols, w, comb, run, near, s_buf, r_buf,
     to_sib, from_sib, mine, p_send, p_recv, own, o_buf,
-    load_sem, st_send, st_recv, w_send, w_recv, n_send, n_recv, p_ssem, p_rsem, o_sem,
+    load_sem, st_send, st_recv, hand_send, w_send, w_recv, n_send, n_recv, p_ssem, p_rsem, o_sem,
 ):
     tokens, width = q.shape[0], q.shape[1] // heads
     stretches = tokens // C
@@ -54,7 +54,7 @@
             ((k_hbm, k), (v_hbm, v), (q_hbm, q), (g_hbm, g), (w_hbm, w.at[0]))
         )
     ]
-    for copy in loads:
+    for copy in loads[:4]:
         copy.start()
 
     barrier = pltpu.get_barrier_semaphore()
@@ -63,11 +63,13 @@
         pl.semaphore_signal(barrier, inc=1, device_id=device, device_id_type=MESH)
     pl.semaphore_wait(barrier, len(everyone))
 
-    w_copy = pltpu.make_async_remote_copy(
-        src_ref=w_hbm, dst_ref=w.at[1], send_sem=w_send, recv_sem=w_recv,
-        device_id=sib, device_id_type=MESH,
-    )
-    w_copy.start()
+    def w_copy(tile):
+        at = pl.ds(pl.multiple_of(tile * TILE, TILE), TILE)
+        return pltpu.make_async_remote_copy(
+            src_ref=w_hbm.at[:, at], dst_ref=w.at[1, :, at],
+            send_sem=w_send.at[tile], recv_sem=w_recv.at[tile],
+            device_id=sib, device_id_type=MESH,
+        )
 
     def state_copy(level, chunk):
         part = pl.ds(chunk * per, per)
@@ -75,6 +77,16 @@
             src_ref=s_buf.at[level, part], dst_ref=r_buf.at[level, part],
             send_sem=st_send.at[level, chunk], recv_sem=st_recv.at[level, chunk],
             device_id=partners[level], device_id_type=MESH,
+        )
+
+    last = ctx_bits - 1
+
+    def hand_copy(chunk):
+        part = pl.ds(chunk * per, per)
+        return pltpu.make_async_remote_copy(
+            src_ref=r_buf.at[last, part], dst_ref=r_buf.at[last, part],
+            send_sem=hand_send.at[chunk], recv_sem=st_recv.at[last, chunk],
+            device_id=partners[0], device_id_type=MESH,
         )
 
     def service(level, chunk):
@@ -84,13 +96,24 @@
             total = run[part] + r_buf[level, part].astype(F32)
             run[part] = total
             s_buf[level + 1, part] = total.astype(BF16)
-            state_copy(level + 1, chunk).start()
+            if level + 1 < last:
+                state_copy(level + 1, chunk).start()
+            else:
+                @pl.when(chunk % 2 == digits[0])
+                def _():
+                    state_copy(last, chunk).start()
 
     def lanes(head):
         return pl.ds(pl.multiple_of(head * width, width), width)
 
     loads[0].wait()
     loads[1].wait()
+
+    @pl.loop(0, tiles)
+    def _(tile):
+        w_copy(tile).start()
+
+    loads[4].start()
 
     @pl.loop(0, CHUNKS)
     def _(chunk):
@@ -128,44 +151,58 @@
         jnp.int32, (C, C), 1
     )
 
+    def attend(duo, odd, head):
+        block = duo * 2 + odd
+        token = pl.ds(pl.multiple_of(block * C, C), C)
+        col = lanes(head)
+        gates = gate_cols[head, token, :]
+        query = q[token, col]
+        scores = lax.dot_general(
+            query, k[token, col], (((1,), (1,)), ((), ())), preferred_element_type=F32
+        )
+        weights = (jnp.where(keep, scores, 0.0) * gates[:, 0:1]).astype(BF16)
+        total = jnp.dot(weights, v[token, col], preferred_element_type=F32)
+        if odd:
+            read = jnp.dot(query, near[head, duo], preferred_element_type=F32)
+            total = total + read * gates[:, 1:2]
+        first = stretches // 2
+        for b in range(1, bits):
+            span = lax.div(duo, 2 ** (b - 1))
+            use = lax.rem(span, 2).astype(F32)
+            read = jnp.dot(
+                query, near[head, first + lax.div(span, 2)], preferred_element_type=F32
+            )
+            total = total + read * (gates[:, b + 1 : b + 2] * use)
+            first += stretches // 2 ** (b + 1)
+        return total
+
+    other = 1 - pair
+
     @pl.loop(0, CHUNKS)
     def _(chunk):
         for inner in range(per):
             head = chunk * per + inner
-            col = lanes(head)
-            for c in range(stretches):
-                token = pl.ds(c * C, C)
-                gates = gate_cols[head, token, :]
-                query = q[token, col]
-                scores = lax.dot_general(
-                    query, k[token, col], (((1,), (1,)), ((), ())), preferred_element_type=F32
-                )
-                weights = (jnp.where(keep, scores, 0.0) * gates[:, 0:1]).astype(BF16)
-                total = jnp.dot(weights, v[token, col], preferred_element_type=F32)
-                for b in range(bits):
-                    block = c // 2**b
-                    if block % 2:
-                        read = jnp.dot(
-                            query, near[head, keys.index((2**b, block - 1))],
-                            preferred_element_type=F32,
-                        )
-                        total = total + read * gates[:, b + 1 : b + 2]
-                comb[token, col] = total
+            for odd in range(2):
+                token = pl.ds(pl.multiple_of((other * 2 + odd) * C, C), C)
+                comb[token, lanes(head)] = attend(other, odd, head)
         for level in range(ctx_bits - 1):
-            if level == 0:
-                service(0, chunk)
-            else:
-                @pl.when(chunk >= level)
-                def _():
-                    service(level, chunk - level)
-
-    for step in range(CHUNKS, CHUNKS + ctx_bits - 2):
-        for level in range(1, ctx_bits - 1):
-            if 0 <= step - level < CHUNKS:
-                service(level, step - level)
-
-    for chunk in range(CHUNKS):
-        service(ctx_bits - 1, chunk)
+            @pl.when((chunk >= level) & (chunk < level + CHUNKS // 2))
+            def _():
+                for inner in range(2):
+                    service(level, (chunk - level) * 2 + inner)
+
+    for step in range(CHUNKS, CHUNKS // 2 + ctx_bits - 2):
+        for level in range(ctx_bits - 1):
+            if 0 <= step - level < CHUNKS // 2:
+                for inner in range(2):
+                    service(level, (step - level) * 2 + inner)
+
+    for half in range(CHUNKS // 2):
+        chunk = half * 2 + digits[0]
+        state_copy(last, chunk).wait_recv()
+        hand_copy(chunk).start()
+    for half in range(CHUNKS // 2):
+        hand_copy(half * 2 + 1 - digits[0]).wait_recv()
 
     scale = [digit.astype(F32) for digit in digits]
 
@@ -211,18 +248,23 @@
             from_sib[n], w[1, :, at], preferred_element_type=F32
         )
 
-    other = 1 - pair
     finish(other * 2 + 1 - core, to_sib.at[0])
     sib_copy(0).start()
     finish(other * 2 + core, mine.at[0])
     loads[4].wait()
-    w_copy.wait_recv()
     sib_copy(0).wait_recv()
 
     @pl.loop(0, tiles)
     def _(tile):
+        w_copy(tile).wait_recv()
         p_send[tile] = project(0, tile).astype(BF16)
         p_copy(tile).start()
+
+    @pl.loop(0, heads)
+    def _(head):
+        for odd in range(2):
+            token = pl.ds(pl.multiple_of((pair * 2 + odd) * C, C), C)
+            comb[token, lanes(head)] = attend(pair, odd, head)
 
     finish(pair * 2 + 1 - core, to_sib.at[1])
     sib_copy(1).start()
@@ -244,15 +286,20 @@
     def _(tile):
         p_copy(tile).wait_send()
         out_copy(tile).wait()
+        w_copy(tile).wait_send()
 
     for n in range(2):
         sib_copy(n).wait_send()
-    w_copy.wait_send()
 
     @pl.loop(0, CHUNKS)
     def _(chunk):
-        for level in range(ctx_bits):
+        for level in range(last):
             state_copy(level, chunk).wait_send()
+
+    for half in range(CHUNKS // 2):
+        chunk = half * 2 + digits[0]
+        state_copy(last, chunk).wait_send()
+        hand_copy(chunk).wait_send()
 
 
 def on_device(query_rows, key_rows, value_rows, level_gate, out_weight):
@@ -293,8 +340,9 @@
             dma((5,)),
             dma((ctx_bits, CHUNKS)),
             dma((ctx_bits, CHUNKS)),
-            dma(()),
-            dma(()),
+            dma((CHUNKS,)),
+            dma((tiles,)),
+            dma((tiles,)),
             dma((2,)),
             dma((2,)),
             dma((tiles,)),

time: 82.6 us -> 81.9 us (level)
  no operation moved by 1% of the time
where the time goes in v2:
time: 81.9 us; the launch traced here: 81.8 us
  Pallas kernels  78.6 us (96%)
  local copies, waits for them, and re-layouts  3.13 us (4%)
    pallas_call x1, Pallas kernels, on_device(): pl.pallas_call(functools.partial(kernel, ctx_bits, heads, levels), out_sh...  78.6 us
    unnamed x1, local copies, waits for them, and re-layouts  3.13 us

profile of v2, /device:TPU:0, one launch (start us, length us, event | category | flops | bytes accessed | tf_op | source)
XLA Modules:
  0.0 81.8 jit_solution(9772759176994233071)
XLA Ops:
  0.0 78.6 %levels_project.1 = bf16[256,4096]{1,0:T(8,128)(2,1)} custom-call(bf16[1024,1024]{1,0:T(8,128)(2,1)} %q_hbm.1, bf16[1024,1024]{1,0:T(8,128)(2,1)} %k_hbm.1, bf16[1024,1024]{1,0:T(8,128)(2,1)} %v_hbm.1, f32[6,8,1024]{2,1,0:T(8,128)} %g_hbm.1, bf16[1024,4096]{1,0:T(8,128)(2,1)} %w_hbm.1), custom_call_target="tpu_custom_call" | custom-call | flops 11542724608 | bytes 20971520 | tf_op jit(solution)/shard_map/levels_project/pallas_call | solution.py:316
  78.6 3.1 %copy.7 = bf16[256,4096]{1,0:T(8,128)(2,1)} copy(bf16[256,4096]{1,0:T(8,128)(2,1)} %levels_project.1) | data formatting | bytes 4194304
